TPU v7x, 256 devices: a whole 4x4x8 slice. The times are simulated.
256 devices in a mesh: ctx: 32 (over x, z), tp: 8 (over y, core).
Axes of the slice: x: 4, y: 4, z: 8, core: 2. Of those that a mesh axis runs over, the one named last changes fastest.
Arguments:
- tokens: bfloat16 [16384, 4096], P('ctx', 'tp'), may hold values from -16 to 16
- query_weight: bfloat16 [4096, 4096], P(None, 'tp'), may hold values from -0.09375 to 0.09375
- key_weight: bfloat16 [4096, 1024], P(None, 'tp'), may hold values from -0.09375 to 0.09375
- value_weight: bfloat16 [4096, 1024], P(None, 'tp'), may hold values from -0.09375 to 0.09375
- out_weight: bfloat16 [4096, 4096], P('tp'), may hold values from -0.09375 to 0.09375
- links: int32 [128, 16], P('ctx'), may hold values from 0 to 127, as said below
- counts: int32 [128], P('ctx'), may hold values from 1 to 16, as said below
- doc_ids: int32 [128], replicated, may hold values from 0 to 31, never falling along the last dimension, each value on 1 to 8 neighbouring positions
Outputs:
- mixed: bfloat16 [16384, 4096], P(('ctx', 'tp'))
Inputs may be any that keep to these rules, and one draw needn't show every extreme that they name: `links`: the first entry of each row is the query block itself; the entries of a row are distinct; every listed block lies within 4 ctx indices of its query block (block index // 4), and some query block of every ctx index lists a block exactly 4 indices away. `counts`: the first query block of each ctx index has 2 or more live slots, and block 0 has 16.
All inputs are finite; a program needn't handle non-finite values.
Results may differ from a plain program's by a relative error of at most 0.017.
Values may be sent and summed in bfloat16 or wider, within the bound.
No kernel may reach another device: no remote copies, remote signals or barrier semaphores. Data moves between devices by JAX's collectives and lax.ppermute only.
A program may use at most 64 MiB of HBM per device.

v0:
```python
import jax
import jax.numpy as jnp
from jax import lax
from jax.sharding import PartitionSpec as P

HEAD_DIM = 128
BLOCK = 128
LINKS = 16
REACH = 4


def from_behind(block, axis, distance):
    devices = range(lax.axis_size(axis))
    route = [(i - distance, i) for i in devices if i - distance in devices]
    return lax.ppermute(block, axis, route)


def local(tokens, query_weight, key_weight, value_weight, out_weight, links, counts, doc_ids):
    row_count = tokens.shape[0]
    query_width = query_weight.shape[1]
    key_width = key_weight.shape[1]
    piece = lax.all_gather(tokens, "tp", axis=1, tiled=True)
    weights = (query_weight, key_weight, value_weight)
    query, keys, values = tuple(
        (jnp.dot(piece, weight, preferred_element_type=jnp.float32) for weight in weights)
    )
    query = query.astype(jnp.bfloat16)
    block_count = row_count // BLOCK
    stacked = (
        jnp.stack([keys, values]).astype(jnp.bfloat16).reshape(2, block_count, BLOCK, key_width)
    )
    position = lax.axis_index("ctx")
    first_block = position * block_count
    pieces = []
    for offset in range(-REACH, REACH + 1):
        if offset == 0:
            pieces.append(stacked)
        else:
            pieces.append(from_behind(stacked, "ctx", -offset))
    source = jnp.concatenate(pieces, axis=1)
    anchor = (position - REACH) * block_count
    chosen = jnp.take(source, links - anchor, axis=1, mode="clip")
    kv_local = key_width // HEAD_DIM
    group = query_width // key_width
    chosen_keys = chosen[0].reshape(block_count, LINKS, BLOCK, kv_local, HEAD_DIM)
    chosen_values = chosen[1].reshape(block_count, LINKS, BLOCK, kv_local, HEAD_DIM)
    query_blocks = query.reshape(block_count, BLOCK, kv_local, group, HEAD_DIM)
    block_total = doc_ids.shape[0]
    table = jnp.arange(block_total, dtype=jnp.int32)
    query_index = first_block + jnp.arange(block_count, dtype=jnp.int32)[:, None]
    doc_key = jnp.sum(jnp.where(links[:, :, None] == table, doc_ids, 0), axis=-1)
    doc_query = jnp.sum(jnp.where(query_index == table[None, :], doc_ids[None, :], 0), axis=-1)[
        :, None
    ]
    live = jnp.arange(LINKS, dtype=jnp.int32)[None, :] < counts[:, None]
    earlier = (links < query_index) | (doc_key != doc_query)
    same = links == query_index
    causal = jnp.arange(BLOCK)[None, :] <= jnp.arange(BLOCK)[:, None]
    allowed = live[:, None, :, None] & (
        earlier[:, None, :, None] | same[:, None, :, None] & causal[None, :, None, :]
    )
    allowed = allowed[:, None, None]
    scores = jnp.einsum(
        "bqhgd,bskhd->bhgqsk", query_blocks, chosen_keys, preferred_element_type=jnp.float32
    ) * HEAD_DIM ** (-0.5)
    scores = jnp.where(allowed, scores, -1e30)
    top = jnp.max(scores, axis=(4, 5), keepdims=True)
    powers = jnp.where(allowed, jnp.exp(scores - top), 0.0)
    total = jnp.sum(powers, axis=(4, 5), keepdims=True)
    weights = (powers / total).astype(jnp.bfloat16)
    attended = jnp.einsum(
        "bhgqsk,bskhd->bqhgd", weights, chosen_values, preferred_element_type=jnp.float32
    )
    attended = attended.astype(jnp.bfloat16).reshape(row_count, query_width)
    return lax.psum_scatter(
        jnp.dot(attended, out_weight, preferred_element_type=jnp.float32).astype(jnp.bfloat16),
        "tp",
        scatter_dimension=0,
        tiled=True,
    )


def solution(mesh):
    placed = (
        P("ctx", "tp"),
        P(None, "tp"),
        P(None, "tp"),
        P(None, "tp"),
        P("tp", None),
        P("ctx", None),
        P("ctx"),
        P(),
    )
    return jax.shard_map(
        local, mesh=mesh, in_specs=placed, out_specs=P(("ctx", "tp"), None), check_vma=False
    )
```

profile of v0, /device:TPU:6, one launch (start us, length us, event | category | flops | bytes accessed | tf_op | source)
XLA Modules:
  0.0 212.3 jit_solution(15246871406914219502)
XLA Ops:
  6.5 0.7 all-gather.2.cloned.1.call-update
  7.3 0.0 reduce-scatter.2.cloned.1.call-start
  7.3 0.7 broadcast_subtract_fusion
  8.0 0.1 reshape.95
  8.1 0.8 select_reduce_fusion.1
  9.0 0.9 select_reduce_fusion
  9.9 0.7 iota_compare_fusion.3
  10.6 0.8 compare_or_fusion
  11.4 3.7 %or_and_fusion = pred[4,128,16,128]{1,3,2,0:T(8,128)(4,1)} fusion(pred[128,128]{0,1:T(8,128)(4,1)S(1)} %iota_compare_fusion, pred[4,16]{1,0:T(4,128)(4,1)S(1)} %get-tuple-element.6, pred[4,16]{1,0:T(4,128)(4,1)S(1)} %get-tuple-element.5, pred[4,16]{1,0:T(4,128)(4,1)S(1)} %iota_compare_fusion.3), kind=kLoop, calls=%fused_computation.9 | loop fusion | flops 3145728 | bytes 1065152 | tf_op jit(solution)/shard_map/and | solution.py:59
  15.0 31.7 %all-gather.2.cloned.1.call-done = bf16[512,4096]{1,0:T(8,128)(2,1)} async-done(((bf16[512,512]{1,0:T(8,128)(2,1)}), bf16[512,4096]{1,0:T(8,128)(2,1)}) %all-gather.2.cloned.1.call-update) | async-done | bytes 4194320 | tf_op jit(solution)/shard_map/all_gather | solution.py:22
  46.7 3.6 %convolution_convert_fusion.2 = bf16[512,128]{1,0:T(8,128)(2,1)S(1)} fusion(bf16[512,4096]{1,0:T(8,128)(2,1)} %all-gather.2.cloned.1.call-done, bf16[4096,128]{1,0:T(8,128)(2,1)S(1)} %copy-done), kind=kOutput, calls=%fused_computation.17 | convolution fusion | flops 536936448 | bytes 5373952 | tf_op jit(solution)/shard_map/dot_general | solution.py:25
  50.3 0.0 copy-start.6
  50.4 1.3 convolution_convert_fusion.3
  51.6 0.7 pad_maximum_fusion
  52.4 7.9 %collective-permute-start.7 = (bf16[2,4,128,128]{3,2,1,0:T(8,128)(2,1)}, bf16[2,4,128,128]{3,2,1,0:T(8,128)(2,1)}, u32[]{:S(2)}, u32[]{:S(2)}) collective-permute-start(bf16[2,4,128,128]{3,2,1,0:T(8,128)(2,1)} %pad_maximum_fusion), channel_id=1, source_target_pairs={{32,0},{40,8},{48,16},{56,24},{64,32},{72,40},{80,48},{88,56},{96,... | collective-permute-start | bytes 786440 | tf_op jit(solution)/shard_map/ppermute | solution.py:15
  60.3 2.2 %collective-permute-start.6 = (bf16[2,4,128,128]{3,2,1,0:T(8,128)(2,1)}, bf16[2,4,128,128]{3,2,1,0:T(8,128)(2,1)}, u32[]{:S(2)}, u32[]{:S(2)}) collective-permute-start(bf16[2,4,128,128]{3,2,1,0:T(8,128)(2,1)} %pad_maximum_fusion), channel_id=1, source_target_pairs={{24,0},{32,8},{40,16},{48,24},{56,32},{64,40},{72,48},{80,56},{88,... | collective-permute-start | bytes 786440 | tf_op jit(solution)/shard_map/ppermute | solution.py:15
  62.5 4.5 %collective-permute-start.2 = (bf16[2,4,128,128]{3,2,1,0:T(8,128)(2,1)}, bf16[2,4,128,128]{3,2,1,0:T(8,128)(2,1)}, u32[]{:S(2)}, u32[]{:S(2)}) collective-permute-start(bf16[2,4,128,128]{3,2,1,0:T(8,128)(2,1)} %pad_maximum_fusion), channel_id=1, source_target_pairs={{0,16},{8,24},{16,32},{24,40},{32,48},{40,56},{48,64},{56,72},{64,... | collective-permute-start | bytes 786440 | tf_op jit(solution)/shard_map/ppermute | solution.py:15
  67.0 5.5 %collective-permute-start.1 = (bf16[2,4,128,128]{3,2,1,0:T(8,128)(2,1)}, bf16[2,4,128,128]{3,2,1,0:T(8,128)(2,1)}, u32[]{:S(2)}, u32[]{:S(2)}) collective-permute-start(bf16[2,4,128,128]{3,2,1,0:T(8,128)(2,1)} %pad_maximum_fusion), channel_id=1, source_target_pairs={{0,24},{8,32},{16,40},{24,48},{32,56},{40,64},{48,72},{56,80},{64,... | collective-permute-start | bytes 786440 | tf_op jit(solution)/shard_map/ppermute | solution.py:15
  72.5 2.0 collective-permute-start
  74.6 2.3 %convolution_convert_fusion.1 = bf16[512,512]{1,0:T(8,128)(2,1)S(1)} fusion(bf16[512,4096]{1,0:T(8,128)(2,1)S(1)} %copy-done.7, bf16[4096,512]{1,0:T(8,128)(2,1)S(1)} %copy-done.6), kind=kOutput, calls=%fused_computation.14 | convolution fusion | flops 2147745792 | bytes 8912896 | tf_op jit(solution)/shard_map/dot_general | solution.py:25
  76.9 0.9 reshape.90
  77.8 32.8 %collective-permute-done = bf16[2,4,128,128]{3,2,1,0:T(8,128)(2,1)S(1)} collective-permute-done((bf16[2,4,128,128]{3,2,1,0:T(8,128)(2,1)}, bf16[2,4,128,128]{3,2,1,0:T(8,128)(2,1)S(1)}, u32[]{:S(2)}, u32[]{:S(2)}) %collective-permute-start) | collective-permute-done | bytes 262176 | tf_op jit(solution)/shard_map/ppermute | solution.py:15
  110.6 0.7 copy-done.5
  111.4 1.9 collective-permute-start.3
  113.3 1.0 constant_dynamic-update-slice_fusion.8
  114.2 0.0 collective-permute-done.1
  114.2 7.4 %collective-permute-start.5 = (bf16[2,4,128,128]{3,2,1,0:T(8,128)(2,1)}, bf16[2,4,128,128]{3,2,1,0:T(8,128)(2,1)S(1)}, u32[]{:S(2)}, u32[]{:S(2)}) collective-permute-start(bf16[2,4,128,128]{3,2,1,0:T(8,128)(2,1)} %pad_maximum_fusion), channel_id=1, source_target_pairs={{16,0},{24,8},{32,16},{40,24},{48,32},{56,40},{64,48},{72,56},{80,... | collective-permute-start | bytes 786440 | tf_op jit(solution)/shard_map/ppermute | solution.py:15
  121.7 1.0 constant_dynamic-update-slice_fusion.7
  122.7 0.0 collective-permute-done.2
  122.7 4.1 %collective-permute-start.4 = (bf16[2,4,128,128]{3,2,1,0:T(8,128)(2,1)}, bf16[2,4,128,128]{3,2,1,0:T(8,128)(2,1)S(1)}, u32[]{:S(2)}, u32[]{:S(2)}) collective-permute-start(bf16[2,4,128,128]{3,2,1,0:T(8,128)(2,1)} %pad_maximum_fusion), channel_id=1, source_target_pairs={{8,0},{16,8},{24,16},{32,24},{40,32},{48,40},{56,48},{64,56},{72,6... | collective-permute-start | bytes 786440 | tf_op jit(solution)/shard_map/ppermute | solution.py:15
  126.8 1.0 constant_dynamic-update-slice_fusion.6
  127.8 0.0 collective-permute-done.3
  127.9 0.9 constant_dynamic-update-slice_fusion.4
  128.8 9.5 %collective-permute-done.4 = bf16[2,4,128,128]{3,2,1,0:T(8,128)(2,1)S(1)} collective-permute-done((bf16[2,4,128,128]{3,2,1,0:T(8,128)(2,1)}, bf16[2,4,128,128]{3,2,1,0:T(8,128)(2,1)S(1)}, u32[]{:S(2)}, u32[]{:S(2)}) %collective-permute-start.4) | collective-permute-done | bytes 262176 | tf_op jit(solution)/shard_map/ppermute | solution.py:15
  138.4 0.0 collective-permute-done.5
  138.4 0.0 collective-permute-done.6
  138.4 1.0 constant_dynamic-update-slice_fusion.1
  139.4 0.0 collective-permute-done.7
  139.4 1.0 constant_dynamic-update-slice_fusion
  140.4 3.0 %gather_fusion = bf16[64,2,128,128]{3,2,1,0:T(8,128)(2,1)} fusion(bf16[2,36,128,128]{3,2,1,0:T(8,128)(2,1)S(1)} %constant_dynamic-update-slice_fusion, s32[1024]{0:T(1024)S(1)} %pad_clamp_fusion), kind=kCustom, calls=%fused_computation | custom fusion | bytes 8388864 | tf_op jit(solution)/shard_map/jit(_take)/gather | solution.py:42
  143.5 2.9 %copy.18 = bf16[64,2,128,128]{3,2,0,1:T(8,128)(2,1)S(1)} copy(bf16[64,2,128,128]{3,2,1,0:T(8,128)(2,1)} %gather_fusion) | data formatting | bytes 8388608 | tf_op jit(solution)/shard_map/jit(_take)/gather | solution.py:42
  146.4 2.6 %fusion = (f32[4,4,128]{2,1,0:T(4,128)S(1)}, f32[4,16,128,128,4]{3,2,4,1,0:T(8,128)S(1)}) fusion(pred[4,128,16,128]{1,3,2,0:T(8,128)(4,1)S(1)} %copy-done.1, bf16[4,128,4,128,1]{3,2,1,0,4:T(4,128)(2,1)S(1)} %bitcast.87, bf16[2,4,16,128,128]{4,3,2,1,0:T(8,128)(2,1)S(1)} %bitcast.85), kind=kOutput, calls=%fused_computation.4 | convolution fusion | flops 1086322688 | bytes 20455424 | tf_op jit(solution)/shard_map/bqhgd,bskhd->bhgqsk/dot_general | solution.py:63
  149.0 4.3 %fusion.1 = f32[4,4,128]{2,1,0:T(4,128)S(1)} fusion(f32[4,16,128,128,4]{3,2,4,1,0:T(8,128)S(1)} %get-tuple-element.8, f32[4,4,128]{2,1,0:T(4,128)S(1)} %get-tuple-element.7, pred[4,128,16,128]{1,3,2,0:T(8,128)(4,1)S(1)} %copy-done.1), kind=kLoop, calls=%fused_computation.5 | loop fusion | flops 20969472 | bytes 17842176 | tf_op jit(solution)/shard_map/reduce_sum | solution.py:69
  153.2 6.3 %fusion.11 = bf16[4,128,1,4,128]{1,4,3,0,2:T(8,128)(2,1)S(1)} fusion(f32[4,4,128]{2,1,0:T(4,128)S(1)} %fusion.1, f32[4,4,128]{2,1,0:T(4,128)S(1)} %get-tuple-element.7, f32[4,16,128,128,4]{3,2,4,1,0:T(8,128)S(1)} %get-tuple-element.8, pred[4,128,16,128]{1,3,2,0:T(8,128)(4,1)S(1)} %copy-done.1, bf16[2,4,16,128,128]{4,3,2,1,0:T(8,128)(2,1)} %bitcast.86), kind=kOutput, calls=%fused_computation.16 | convolution fusion | flops 1099169792 | bytes 20463616 | tf_op jit(solution)/shard_map/bhgqsk,bskhd->bqhgd/dot_general | solution.py:71
  159.5 0.3 copy.22
  159.8 6.5 %convolution_convert_fusion = bf16[512,4096]{1,0:T(8,128)(2,1)} fusion(bf16[512,4096]{1,0:T(8,128)(2,1)} %param.12, bf16[64,8,4,128]{3,2,1,0:T(4,128)(2,1)S(1)} %bitcast.88), kind=kOutput, calls=%fused_computation.8 | convolution fusion | flops 2149580800 | bytes 8912896 | tf_op jit(solution)/shard_map/dot_general | solution.py:76
  166.3 0.0 reduce-scatter.2.cloned.1.call-update
  166.3 39.1 %reduce-scatter.2.cloned.1.call-done = bf16[64,4096]{1,0:T(8,128)(2,1)} async-done(((bf16[512,4096]{1,0:T(8,128)(2,1)}), bf16[64,4096]{1,0:T(8,128)(2,1)}) %reduce-scatter.2.cloned.1.call-update) | async-done | bytes 524304 | tf_op jit(solution)/shard_map/reduce_scatter | solution.py:75
  (23 shorter events, 0.2 us)
Async XLA Ops:
  6.5 40.2 %copy-start = (bf16[4096,128]{1,0:T(8,128)(2,1)S(1)}, bf16[4096,128]{1,0:T(8,128)(2,1)}, u32[]{:S(2)}) copy-start(bf16[4096,128]{1,0:T(8,128)(2,1)} %param.11) | copy-start | bytes 3145732
  6.5 43.8 %copy-start.8 = (bf16[4096,128]{1,0:T(8,128)(2,1)S(1)}, bf16[4096,128]{1,0:T(8,128)(2,1)}, u32[]{:S(2)}) copy-start(bf16[4096,128]{1,0:T(8,128)(2,1)} %param.10) | copy-start | bytes 3145732
  6.5 40.2 %all-gather.2.cloned.1.call-start = ((), (), s32[]{:S(2)}) async-start(), calls=%async_computation.1 | async-start | bytes 4718592 | tf_op jit(solution)/shard_map/all_gather | solution.py:22
  7.3 198.2 %reduce-scatter.2.cloned.1.call-start = ((), (), s32[]{:S(2)}) async-start(), calls=%async_computation.2 | async-start | bytes 4718592 | tf_op jit(solution)/shard_map/reduce_scatter | solution.py:75
  46.7 3.6 %copy-start.7 = (bf16[512,4096]{1,0:T(8,128)(2,1)S(1)}, bf16[512,4096]{1,0:T(8,128)(2,1)}, u32[]{:S(2)}) copy-start(bf16[512,4096]{1,0:T(8,128)(2,1)} %all-gather.2.cloned.1.call-done) | copy-start | bytes 12582916
  50.3 24.2 %copy-start.6 = (bf16[4096,512]{1,0:T(8,128)(2,1)S(1)}, bf16[4096,512]{1,0:T(8,128)(2,1)}, u32[]{:S(2)}) copy-start(bf16[4096,512]{1,0:T(8,128)(2,1)} %param.9) | copy-start | bytes 12582916
  51.6 20.9 %copy-start.4 = (bf16[512,128]{1,0:T(8,128)(2,1)}, bf16[512,128]{1,0:T(8,128)(2,1)S(1)}, u32[]{:S(2)}) copy-start(bf16[512,128]{1,0:T(8,128)(2,1)S(1)} %convolution_convert_fusion.3) | copy-start | bytes 393220
  52.4 87.0 %collective-permute-start.7 = (bf16[2,4,128,128]{3,2,1,0:T(8,128)(2,1)}, bf16[2,4,128,128]{3,2,1,0:T(8,128)(2,1)}, u32[]{:S(2)}, u32[]{:S(2)}) collective-permute-start(bf16[2,4,128,128]{3,2,1,0:T(8,128)(2,1)} %pad_maximum_fusion), channel_id=1, source_target_pairs={{32,0},{40,8},{48,16},{56,24},{64,32},{72,40},{80,48},{88,56},{96,... | collective-permute-start | bytes 786440 | tf_op jit(solution)/shard_map/ppermute | solution.py:15
  60.3 78.1 %collective-permute-start.6 = (bf16[2,4,128,128]{3,2,1,0:T(8,128)(2,1)}, bf16[2,4,128,128]{3,2,1,0:T(8,128)(2,1)}, u32[]{:S(2)}, u32[]{:S(2)}) collective-permute-start(bf16[2,4,128,128]{3,2,1,0:T(8,128)(2,1)} %pad_maximum_fusion), channel_id=1, source_target_pairs={{24,0},{32,8},{40,16},{48,24},{56,32},{64,40},{72,48},{80,56},{88,... | collective-permute-start | bytes 786440 | tf_op jit(solution)/shard_map/ppermute | solution.py:15
  62.5 60.2 %collective-permute-start.2 = (bf16[2,4,128,128]{3,2,1,0:T(8,128)(2,1)}, bf16[2,4,128,128]{3,2,1,0:T(8,128)(2,1)}, u32[]{:S(2)}, u32[]{:S(2)}) collective-permute-start(bf16[2,4,128,128]{3,2,1,0:T(8,128)(2,1)} %pad_maximum_fusion), channel_id=1, source_target_pairs={{0,16},{8,24},{16,32},{24,40},{32,48},{40,56},{48,64},{56,72},{64,... | collective-permute-start | bytes 786440 | tf_op jit(solution)/shard_map/ppermute | solution.py:15
  67.0 47.3 %collective-permute-start.1 = (bf16[2,4,128,128]{3,2,1,0:T(8,128)(2,1)}, bf16[2,4,128,128]{3,2,1,0:T(8,128)(2,1)}, u32[]{:S(2)}, u32[]{:S(2)}) collective-permute-start(bf16[2,4,128,128]{3,2,1,0:T(8,128)(2,1)} %pad_maximum_fusion), channel_id=1, source_target_pairs={{0,24},{8,32},{16,40},{24,48},{32,56},{40,64},{48,72},{56,80},{64,... | collective-permute-start | bytes 786440 | tf_op jit(solution)/shard_map/ppermute | solution.py:15
  72.5 38.1 %collective-permute-start = (bf16[2,4,128,128]{3,2,1,0:T(8,128)(2,1)}, bf16[2,4,128,128]{3,2,1,0:T(8,128)(2,1)S(1)}, u32[]{:S(2)}, u32[]{:S(2)}) collective-permute-start(bf16[2,4,128,128]{3,2,1,0:T(8,128)(2,1)} %pad_maximum_fusion), channel_id=1, source_target_pairs={{0,32},{8,40},{16,48},{24,56},{32,64},{40,72},{48,80},{56,88},{64,... | collective-permute-start | bytes 786440 | tf_op jit(solution)/shard_map/ppermute | solution.py:15
  110.6 0.7 copy-start.5
  111.4 16.5 %collective-permute-start.3 = (bf16[2,4,128,128]{3,2,1,0:T(8,128)(2,1)}, bf16[2,4,128,128]{3,2,1,0:T(8,128)(2,1)S(1)}, u32[]{:S(2)}, u32[]{:S(2)}) collective-permute-start(bf16[2,4,128,128]{3,2,1,0:T(8,128)(2,1)} %pad_maximum_fusion), channel_id=1, source_target_pairs={{0,8},{8,16},{16,24},{24,32},{32,40},{40,48},{48,56},{56,64},{64,7... | collective-permute-start | bytes 786440 | tf_op jit(solution)/shard_map/ppermute | solution.py:15
  114.2 24.1 %collective-permute-start.5 = (bf16[2,4,128,128]{3,2,1,0:T(8,128)(2,1)}, bf16[2,4,128,128]{3,2,1,0:T(8,128)(2,1)S(1)}, u32[]{:S(2)}, u32[]{:S(2)}) collective-permute-start(bf16[2,4,128,128]{3,2,1,0:T(8,128)(2,1)} %pad_maximum_fusion), channel_id=1, source_target_pairs={{16,0},{24,8},{32,16},{40,24},{48,32},{56,40},{64,48},{72,56},{80,... | collective-permute-start | bytes 786440 | tf_op jit(solution)/shard_map/ppermute | solution.py:15
  122.7 15.6 %collective-permute-start.4 = (bf16[2,4,128,128]{3,2,1,0:T(8,128)(2,1)}, bf16[2,4,128,128]{3,2,1,0:T(8,128)(2,1)S(1)}, u32[]{:S(2)}, u32[]{:S(2)}) collective-permute-start(bf16[2,4,128,128]{3,2,1,0:T(8,128)(2,1)} %pad_maximum_fusion), channel_id=1, source_target_pairs={{8,0},{16,8},{24,16},{32,24},{40,32},{48,40},{56,48},{64,56},{72,6... | collective-permute-start | bytes 786440 | tf_op jit(solution)/shard_map/ppermute | solution.py:15
  143.4 2.9 %copy-start.1 = (pred[4,128,16,128]{1,3,2,0:T(8,128)(4,1)S(1)}, pred[4,128,16,128]{1,3,2,0:T(8,128)(4,1)}, u32[]{:S(2)}) copy-start(pred[4,128,16,128]{1,3,2,0:T(8,128)(4,1)} %or_and_fusion) | copy-start | bytes 3145732
  143.5 2.9 %copy-start.3 = (bf16[4,128,4,128]{3,2,1,0:T(4,128)(2,1)S(1)}, bf16[4,128,4,128]{3,2,1,0:T(4,128)(2,1)}, u32[]{:S(2)}) copy-start(bf16[4,128,4,128]{3,2,1,0:T(4,128)(2,1)} %reshape.90) | copy-start | bytes 1572868
  146.3 2.6 %copy-start.2 = (bf16[64,2,128,128]{3,2,0,1:T(8,128)(2,1)}, bf16[64,2,128,128]{3,2,0,1:T(8,128)(2,1)S(1)}, u32[]{:S(2)}) copy-start(bf16[64,2,128,128]{3,2,0,1:T(8,128)(2,1)S(1)} %copy.18) | copy-start | bytes 12582916
Sparse Core Ops, SparseCore 0:
  9.2 37.5 all-gather.1
  166.5 38.9 reduce-scatter.1
where the time goes:
time: 213 us; the launch traced here: 212 us
  waiting for transfers between devices  114 us (54%)
  starting transfers between devices  35.6 us (17%)
  matrix products  22.5 us (11%)
  between operations  13.7 us (6%)
  other arithmetic  13.6 us (6%)
  local copies, waits for them, and re-layouts  13 us (6%)
    ppermute x8, waiting for transfers between devices, from_behind(): return lax.ppermute(block, axis, route)  42.4 us
    reduce_scatter x1, waiting for transfers between devices, local(): lax.psum_scatter(jnp.dot(attended, out_weight, preferred_element_type=jnp...  39.1 us
    ppermute x8, starting transfers between devices, from_behind(): return lax.ppermute(block, axis, route)  35.6 us
    all_gather x1, waiting for transfers between devices, local(): piece = lax.all_gather(tokens, 'tp', axis=1, tiled=True)  31.7 us
    dot_general x3, matrix products, local(): jnp.dot(piece, weight, preferred_element_type=jnp.float32)  7.17 us
    dot_general x1, matrix products, local(): jnp.dot(attended, out_weight, preferred_element_type=jnp.float32)  6.49 us
    dot_general x1, matrix products, local(): jnp.einsum('bhgqsk,bskhd->bqhgd', weights, chosen_values, preferred_eleme...  6.27 us
    gather x2, local copies, waits for them, and re-layouts, local(): chosen = jnp.take(source, links - anchor, axis=1, mode='clip')  5.91 us
  transfers between devices with their start and end apart: 10, of which 4 were waited for; matrix products, arithmetic and copies ran while one was open for 8% of the time, Pallas kernels for 0%

commit v1 on v0

--- a/solution.py
+++ b/solution.py
@@ -1,3 +1,4 @@
+import functools
 import jax
 import jax.numpy as jnp
 from jax import lax
@@ -7,6 +8,15 @@
 BLOCK = 128
 LINKS = 16
 REACH = 4
+
+
+def _finish_column(arr_in, axis_name):
+    return jnp.concatenate(
+        lax.all_to_all(jnp.stack([arr_in] * lax.axis_size(axis_name)), axis_name, 0, 0), axis=1
+    )
+
+
+draw_the_strips_all = functools.partial(_finish_column, axis_name="tp")
 
 
 def from_behind(block, axis, distance):
@@ -19,7 +29,7 @@
     row_count = tokens.shape[0]
     query_width = query_weight.shape[1]
     key_width = key_weight.shape[1]
-    piece = lax.all_gather(tokens, "tp", axis=1, tiled=True)
+    piece = draw_the_strips_all(tokens)
     weights = (query_weight, key_weight, value_weight)
     query, keys, values = tuple(
         (jnp.dot(piece, weight, preferred_element_type=jnp.float32) for weight in weights)

time: 213 us -> 244 us (1.15)
  local copies, waits for them, and re-layouts: 13 us -> 36 us
  other arithmetic: 13.6 us -> 9.29 us
  waiting for transfers between devices: 114 us -> 118 us
  starting transfers between devices: 35.6 us -> 39.4 us
  matrix products: 22.5 us -> 26.1 us
    all_to_all x0 -> x1, waiting for transfers between devices: none -> 45.3 us  [_finish_column(): lax.all_to_all(jnp.stack([arr_in] * lax.axis_size(axis_name)), axis_name,...]
    all_gather x1 -> x0, waiting for transfers between devices: 31.7 us -> none  [local(): piece = lax.all_gather(tokens, 'tp', axis=1, tiled=True)]
    another operation x1 -> x3, local copies, waits for them, and re-layouts: 0.92 us -> 11.8 us
    all_to_all x0 -> x1, local copies, waits for them, and re-layouts: none -> 6.52 us  [_finish_column(): lax.all_to_all(jnp.stack([arr_in] * lax.axis_size(axis_name)), axis_name,...]
    reshape x0 -> x1, local copies, waits for them, and re-layouts: none -> 6.49 us  [_finish_column(): jnp.concatenate(lax.all_to_all(jnp.stack([arr_in] * lax.axis_size(axis_na...]
    ppermute x8, waiting for transfers between devices: 42.4 us -> 36.8 us  [from_behind(): return lax.ppermute(block, axis, route)]
    all_to_all x0 -> x1, starting transfers between devices: none -> 4.67 us  [_finish_column(): lax.all_to_all(jnp.stack([arr_in] * lax.axis_size(axis_name)), axis_name,...]
    dot_general x3, matrix products: 7.17 us -> 10.6 us  [local(): jnp.dot(piece, weight, preferred_element_type=jnp.float32)]
  transfers between devices with their start and end apart: 10 -> 10, of which waited for: 4 -> 4; matrix products, arithmetic and copies ran while one was open for 8% -> 9% of each run, Pallas kernels for 0% -> 0%
where the time goes in v1:
time: 244 us; the launch traced here: 243 us
  waiting for transfers between devices  118 us (48%)
  starting transfers between devices  39.4 us (16%)
  local copies, waits for them, and re-layouts  36 us (15%)
  matrix products  26.1 us (11%)
  between operations  13.7 us (6%)
  other arithmetic  9.29 us (4%)
    all_to_all x1, waiting for transfers between devices, _finish_column(): lax.all_to_all(jnp.stack([arr_in] * lax.axis_size(axis_name)), axis_name,...  45.3 us
    ppermute x8, waiting for transfers between devices, from_behind(): return lax.ppermute(block, axis, route)  36.8 us
    reduce_scatter x1, waiting for transfers between devices, local(): lax.psum_scatter(jnp.dot(attended, out_weight, preferred_element_type=jnp...  36.3 us
    ppermute x8, starting transfers between devices, from_behind(): return lax.ppermute(block, axis, route)  34.7 us
    dot_general x3, matrix products, local(): jnp.dot(piece, weight, preferred_element_type=jnp.float32)  10.6 us
    another operation x2, local copies, waits for them, and re-layouts  8.31 us
    dot_general x1, matrix products, local(): jnp.dot(attended, out_weight, preferred_element_type=jnp.float32)  6.58 us
    all_to_all x1, local copies, waits for them, and re-layouts, _finish_column(): lax.all_to_all(jnp.stack([arr_in] * lax.axis_size(axis_name)), axis_name,...  6.52 us
  transfers between devices with their start and end apart: 10, of which 4 were waited for; matrix products, arithmetic and copies ran while one was open for 9% of the time, Pallas kernels for 0%

profile of v1, /device:TPU:6, one launch (start us, length us, event | category | flops | bytes accessed | tf_op | source)
XLA Modules:
  0.0 243.0 jit_solution(17653229663786581388)
XLA Ops:
  6.5 3.5 %stack.4 = bf16[8,512,512]{2,1,0:T(8,128)(2,1)} broadcast(bf16[512,512]{1,0:T(8,128)(2,1)} %param.8), dimensions={1,2} | broadcast | bytes 4718592 | tf_op jit(solution)/shard_map/stack | solution.py:15
  10.0 4.7 %all-to-all-start = ((bf16[8,512,512]{2,1,0:T(8,128)(2,1)}), bf16[8,512,512]{2,1,0:T(8,128)(2,1)}, u32[]{:S(2)}, u32[]{:S(2)}) async-start(bf16[8,512,512]{2,1,0:T(8,128)(2,1)} %stack.4), calls=%async_computation | async-start | bytes 8388608 | tf_op jit(solution)/shard_map/all_to_all | solution.py:15
  14.7 0.0 reduce-scatter.2.cloned.1.call-start
  14.8 0.1 reshape.118
  14.9 0.2 select_reduce_fusion.1
  15.1 0.2 select_reduce_fusion
  15.3 0.1 compare_or_fusion
  15.4 3.7 %or_and_fusion = pred[4,128,16,128]{1,3,2,0:T(8,128)(4,1)} fusion(pred[128,128]{0,1:T(8,128)(4,1)S(1)} %iota_compare_fusion, pred[4,16]{1,0:T(4,128)(4,1)S(1)} %get-tuple-element.6, pred[4,16]{1,0:T(4,128)(4,1)S(1)} %get-tuple-element.5, pred[4,16]{1,0:T(4,128)(4,1)S(1)} %get-tuple-element.9), kind=kLoop, calls=%fused_computation.10 | loop fusion | flops 3145728 | bytes 1065152 | tf_op jit(solution)/shard_map/and | solution.py:69
  19.1 45.3 %all-to-all-done = bf16[8,512,512]{2,1,0:T(8,128)(2,1)} async-done(((bf16[8,512,512]{2,1,0:T(8,128)(2,1)}), bf16[8,512,512]{2,1,0:T(8,128)(2,1)}, u32[]{:S(2)}, u32[]{:S(2)}) %all-to-all-start) | async-done | bytes 4194336 | tf_op jit(solution)/shard_map/all_to_all | solution.py:15
  64.3 6.5 %copy.32 = bf16[512,8,512]{2,1,0:T(8,128)(2,1)} copy(bf16[512,8,512]{2,0,1:T(8,128)(2,1)} %bitcast.1) | data formatting | bytes 8388608 | tf_op jit(solution)/shard_map/reshape | solution.py:14
  70.8 7.4 %reshape.109 = bf16[4,128,4096]{2,1,0:T(8,128)(2,1)} reshape(bf16[512,8,512]{2,1,0:T(8,128)(2,1)} %copy.32) | data formatting | bytes 8388608 | tf_op jit(solution)/shard_map/reshape.78
  78.2 3.6 %fusion.15 = bf16[1,4,128,128]{3,2,1,0:T(8,128)(2,1)S(1)} fusion(bf16[4,128,4096]{2,1,0:T(8,128)(2,1)} %reshape.109, bf16[4096,128]{1,0:T(8,128)(2,1)S(1)} %copy-done), kind=kOutput, calls=%fused_computation.21 | convolution fusion | flops 536936448 | bytes 5373952 | tf_op jit(solution)/shard_map/dot_general | solution.py:35
  81.8 0.1 copy-done.10
  82.0 1.2 fusion.14
  83.2 0.7 pad_maximum_fusion
  84.0 9.3 %collective-permute-start.7 = (bf16[2,4,128,128]{3,2,1,0:T(8,128)(2,1)}, bf16[2,4,128,128]{3,2,1,0:T(8,128)(2,1)S(1)}, u32[]{:S(2)}, u32[]{:S(2)}) collective-permute-start(bf16[2,4,128,128]{3,2,1,0:T(8,128)(2,1)} %pad_maximum_fusion), channel_id=1, source_target_pairs={{32,0},{40,8},{48,16},{56,24},{64,32},{72,40},{80,48},{88,56},{96,... | collective-permute-start | bytes 786440 | tf_op jit(solution)/shard_map/ppermute | solution.py:25
  93.3 1.9 collective-permute-start.6
  95.3 4.4 %collective-permute-start.2 = (bf16[2,4,128,128]{3,2,1,0:T(8,128)(2,1)}, bf16[2,4,128,128]{3,2,1,0:T(8,128)(2,1)}, u32[]{:S(2)}, u32[]{:S(2)}) collective-permute-start(bf16[2,4,128,128]{3,2,1,0:T(8,128)(2,1)} %pad_maximum_fusion), channel_id=1, source_target_pairs={{0,16},{8,24},{16,32},{24,40},{32,48},{40,56},{48,64},{56,72},{64,... | collective-permute-start | bytes 786440 | tf_op jit(solution)/shard_map/ppermute | solution.py:25
  99.6 6.7 %collective-permute-start.1 = (bf16[2,4,128,128]{3,2,1,0:T(8,128)(2,1)}, bf16[2,4,128,128]{3,2,1,0:T(8,128)(2,1)}, u32[]{:S(2)}, u32[]{:S(2)}) collective-permute-start(bf16[2,4,128,128]{3,2,1,0:T(8,128)(2,1)} %pad_maximum_fusion), channel_id=1, source_target_pairs={{0,24},{8,32},{16,40},{24,48},{32,56},{40,64},{48,72},{56,80},{64,... | collective-permute-start | bytes 786440 | tf_op jit(solution)/shard_map/ppermute | solution.py:25
  106.3 2.4 collective-permute-start
  108.7 6.5 %copy.31 = bf16[8,512,512]{1,2,0:T(8,128)(2,1)} copy(bf16[8,512,512]{2,1,0:T(8,128)(2,1)} %all-to-all-done) | data formatting | bytes 8388608 | tf_op jit(solution)/shard_map/all_to_all | solution.py:15
  115.2 5.8 %convolution_convert_fusion.1 = bf16[512,512]{1,0:T(8,128)(2,1)S(1)} fusion(bf16[512,4096]{0,1:T(8,128)(2,1)} %bitcast.99, bf16[4096,512]{1,0:T(8,128)(2,1)} %param.9), kind=kOutput, calls=%fused_computation.15 | convolution fusion | flops 2147745792 | bytes 8912896 | tf_op jit(solution)/shard_map/dot_general | solution.py:35
  121.0 0.9 reshape.113
  121.9 25.4 %collective-permute-done = bf16[2,4,128,128]{3,2,1,0:T(8,128)(2,1)S(1)} collective-permute-done((bf16[2,4,128,128]{3,2,1,0:T(8,128)(2,1)}, bf16[2,4,128,128]{3,2,1,0:T(8,128)(2,1)S(1)}, u32[]{:S(2)}, u32[]{:S(2)}) %collective-permute-start) | collective-permute-done | bytes 262176 | tf_op jit(solution)/shard_map/ppermute | solution.py:25
  147.3 0.7 copy-done.6
  148.0 1.9 collective-permute-start.3
  149.9 1.0 constant_dynamic-update-slice_fusion.8
  150.9 0.0 collective-permute-done.1
  150.9 1.9 collective-permute-start.5
  152.8 1.0 constant_dynamic-update-slice_fusion.7
  153.8 0.0 collective-permute-done.2
  153.8 6.2 %collective-permute-start.4 = (bf16[2,4,128,128]{3,2,1,0:T(8,128)(2,1)}, bf16[2,4,128,128]{3,2,1,0:T(8,128)(2,1)S(1)}, u32[]{:S(2)}, u32[]{:S(2)}) collective-permute-start(bf16[2,4,128,128]{3,2,1,0:T(8,128)(2,1)} %pad_maximum_fusion), channel_id=1, source_target_pairs={{8,0},{16,8},{24,16},{32,24},{40,32},{48,40},{56,48},{64,56},{72,6... | collective-permute-start | bytes 786440 | tf_op jit(solution)/shard_map/ppermute | solution.py:25
  160.1 1.0 constant_dynamic-update-slice_fusion.6
  161.1 0.0 collective-permute-done.3
  161.2 11.4 %collective-permute-done.4 = bf16[2,4,128,128]{3,2,1,0:T(8,128)(2,1)S(1)} collective-permute-done((bf16[2,4,128,128]{3,2,1,0:T(8,128)(2,1)}, bf16[2,4,128,128]{3,2,1,0:T(8,128)(2,1)S(1)}, u32[]{:S(2)}, u32[]{:S(2)}) %collective-permute-start.4) | collective-permute-done | bytes 262176 | tf_op jit(solution)/shard_map/ppermute | solution.py:25
  172.6 0.0 collective-permute-done.5
  172.7 1.0 constant_dynamic-update-slice_fusion.1
  173.6 0.0 collective-permute-done.7
  173.7 3.0 %gather_fusion = bf16[64,2,128,128]{3,2,1,0:T(8,128)(2,1)} fusion(bf16[2,36,128,128]{3,2,1,0:T(8,128)(2,1)S(1)} %constant_dynamic-update-slice_fusion, s32[1024]{0:T(1024)S(1)} %pad_clamp_fusion), kind=kCustom, calls=%fused_computation | custom fusion | bytes 8388864 | tf_op jit(solution)/shard_map/jit(_take)/gather | solution.py:52
  176.7 2.9 %copy.59 = bf16[4,16,2,128,128]{4,3,1,0,2:T(8,128)(2,1)S(1)} copy(bf16[4,16,2,128,128]{4,3,2,1,0:T(8,128)(2,1)} %bitcast.96) | data formatting | bytes 8388608 | tf_op jit(solution)/shard_map/jit(_take)/gather | solution.py:52
  179.7 2.6 %fusion = (f32[4,4,128]{2,1,0:T(4,128)S(1)}, f32[4,16,128,128,4]{3,2,4,1,0:T(8,128)S(1)}) fusion(pred[4,128,16,128]{1,3,2,0:T(8,128)(4,1)S(1)} %copy-done.2, bf16[4,128,4,128,1]{3,2,1,0,4:T(4,128)(2,1)S(1)} %bitcast.100, bf16[2,4,16,128,128]{4,3,2,1,0:T(8,128)(2,1)S(1)} %bitcast.97), kind=kOutput, calls=%fused_computation.4 | convolution fusion | flops 1086322688 | bytes 20455424 | tf_op jit(solution)/shard_map/bqhgd,bskhd->bhgqsk/dot_general | solution.py:73
  182.2 4.3 %fusion.1 = f32[4,4,128]{2,1,0:T(4,128)S(1)} fusion(f32[4,16,128,128,4]{3,2,4,1,0:T(8,128)S(1)} %get-tuple-element.8, f32[4,4,128]{2,1,0:T(4,128)S(1)} %get-tuple-element.7, pred[4,128,16,128]{1,3,2,0:T(8,128)(4,1)S(1)} %copy-done.2), kind=kLoop, calls=%fused_computation.5 | loop fusion | flops 20969472 | bytes 17842176 | tf_op jit(solution)/shard_map/reduce_sum | solution.py:79
  186.6 6.3 %fusion.11 = bf16[4,128,1,4,128]{1,4,3,0,2:T(8,128)(2,1)S(1)} fusion(f32[4,4,128]{2,1,0:T(4,128)S(1)} %fusion.1, f32[4,4,128]{2,1,0:T(4,128)S(1)} %get-tuple-element.7, f32[4,16,128,128,4]{3,2,4,1,0:T(8,128)S(1)} %get-tuple-element.8, pred[4,128,16,128]{1,3,2,0:T(8,128)(4,1)S(1)} %copy-done.2, bf16[2,4,16,128,128]{4,3,2,1,0:T(8,128)(2,1)} %bitcast.98), kind=kOutput, calls=%fused_computation.17 | convolution fusion | flops 1099169792 | bytes 20463616 | tf_op jit(solution)/shard_map/bhgqsk,bskhd->bqhgd/dot_general | solution.py:81
  192.9 0.3 copy.37
  193.2 0.0 copy-start.1
  193.2 6.6 %convolution_convert_fusion = bf16[512,4096]{1,0:T(8,128)(2,1)} fusion(bf16[512,4096]{1,0:T(8,128)(2,1)} %param.12, bf16[64,8,4,128]{3,2,1,0:T(4,128)(2,1)S(1)} %bitcast.101), kind=kOutput, calls=%fused_computation.8 | convolution fusion | flops 2149580800 | bytes 8912896 | tf_op jit(solution)/shard_map/dot_general | solution.py:86
  199.8 0.0 reduce-scatter.2.cloned.1.call-update
  199.8 36.3 %reduce-scatter.2.cloned.1.call-done = bf16[64,4096]{1,0:T(8,128)(2,1)} async-done(((bf16[512,4096]{1,0:T(8,128)(2,1)}), bf16[64,4096]{1,0:T(8,128)(2,1)}) %reduce-scatter.2.cloned.1.call-update) | async-done | bytes 524304 | tf_op jit(solution)/shard_map/reduce_scatter | solution.py:85
  (29 shorter events, 0.2 us)
Async XLA Ops:
  6.5 71.7 %copy-start = (bf16[4096,128]{1,0:T(8,128)(2,1)S(1)}, bf16[4096,128]{1,0:T(8,128)(2,1)}, u32[]{:S(2)}) copy-start(bf16[4096,128]{1,0:T(8,128)(2,1)} %param.11) | copy-start | bytes 3145732
  10.0 4.7 %copy-start.7 = (s32[4,16]{1,0:T(4,128)S(1)}, s32[4,16]{1,0:T(4,128)}, u32[]{:S(2)}) copy-start(s32[4,16]{1,0:T(4,128)} %param.13) | copy-start | bytes 772
  10.0 4.9 %copy-start.9 = (s32[128]{0:T(128)S(1)}, s32[128]{0:T(128)}, u32[]{:S(2)}) copy-start(s32[128]{0:T(128)} %param.15) | copy-start | bytes 1540
  10.0 5.3 %copy-start.8 = (s32[4]{0:T(128)S(1)}, s32[4]{0:T(128)}, u32[]{:S(2)}) copy-start(s32[4]{0:T(128)} %param.14) | copy-start | bytes 52
  10.0 54.3 %all-to-all-start = ((bf16[8,512,512]{2,1,0:T(8,128)(2,1)}), bf16[8,512,512]{2,1,0:T(8,128)(2,1)}, u32[]{:S(2)}, u32[]{:S(2)}) async-start(bf16[8,512,512]{2,1,0:T(8,128)(2,1)} %stack.4), calls=%async_computation | async-start | bytes 8388608 | tf_op jit(solution)/shard_map/all_to_all | solution.py:15
  14.7 221.5 %reduce-scatter.2.cloned.1.call-start = ((), (), s32[]{:S(2)}) async-start(), calls=%async_computation.2 | async-start | bytes 4718592 | tf_op jit(solution)/shard_map/reduce_scatter | solution.py:85
  78.2 3.6 %copy-start.4 = (bf16[4,128,4096]{2,1,0:T(8,128)(2,1)S(1)}, bf16[4,128,4096]{2,1,0:T(8,128)(2,1)}, u32[]{:S(2)}) copy-start(bf16[4,128,4096]{2,1,0:T(8,128)(2,1)} %reshape.109) | copy-start | bytes 12582916
  78.2 3.7 %copy-start.10 = (bf16[4096,128]{1,0:T(8,128)(2,1)S(1)}, bf16[4096,128]{1,0:T(8,128)(2,1)}, u32[]{:S(2)}) copy-start(bf16[4096,128]{1,0:T(8,128)(2,1)} %param.10) | copy-start | bytes 3145732
  84.0 89.7 %collective-permute-start.7 = (bf16[2,4,128,128]{3,2,1,0:T(8,128)(2,1)}, bf16[2,4,128,128]{3,2,1,0:T(8,128)(2,1)S(1)}, u32[]{:S(2)}, u32[]{:S(2)}) collective-permute-start(bf16[2,4,128,128]{3,2,1,0:T(8,128)(2,1)} %pad_maximum_fusion), channel_id=1, source_target_pairs={{32,0},{40,8},{48,16},{56,24},{64,32},{72,40},{80,48},{88,56},{96,... | collective-permute-start | bytes 786440 | tf_op jit(solution)/shard_map/ppermute | solution.py:25
  93.3 79.3 %collective-permute-start.6 = (bf16[2,4,128,128]{3,2,1,0:T(8,128)(2,1)}, bf16[2,4,128,128]{3,2,1,0:T(8,128)(2,1)}, u32[]{:S(2)}, u32[]{:S(2)}) collective-permute-start(bf16[2,4,128,128]{3,2,1,0:T(8,128)(2,1)} %pad_maximum_fusion), channel_id=1, source_target_pairs={{24,0},{32,8},{40,16},{48,24},{56,32},{64,40},{72,48},{80,56},{88,... | collective-permute-start | bytes 786440 | tf_op jit(solution)/shard_map/ppermute | solution.py:25
  95.3 58.6 %collective-permute-start.2 = (bf16[2,4,128,128]{3,2,1,0:T(8,128)(2,1)}, bf16[2,4,128,128]{3,2,1,0:T(8,128)(2,1)}, u32[]{:S(2)}, u32[]{:S(2)}) collective-permute-start(bf16[2,4,128,128]{3,2,1,0:T(8,128)(2,1)} %pad_maximum_fusion), channel_id=1, source_target_pairs={{0,16},{8,24},{16,32},{24,40},{32,48},{40,56},{48,64},{56,72},{64,... | collective-permute-start | bytes 786440 | tf_op jit(solution)/shard_map/ppermute | solution.py:25
  99.6 51.3 %collective-permute-start.1 = (bf16[2,4,128,128]{3,2,1,0:T(8,128)(2,1)}, bf16[2,4,128,128]{3,2,1,0:T(8,128)(2,1)}, u32[]{:S(2)}, u32[]{:S(2)}) collective-permute-start(bf16[2,4,128,128]{3,2,1,0:T(8,128)(2,1)} %pad_maximum_fusion), channel_id=1, source_target_pairs={{0,24},{8,32},{16,40},{24,48},{32,56},{40,64},{48,72},{56,80},{64,... | collective-permute-start | bytes 786440 | tf_op jit(solution)/shard_map/ppermute | solution.py:25
  106.3 41.0 %collective-permute-start = (bf16[2,4,128,128]{3,2,1,0:T(8,128)(2,1)}, bf16[2,4,128,128]{3,2,1,0:T(8,128)(2,1)S(1)}, u32[]{:S(2)}, u32[]{:S(2)}) collective-permute-start(bf16[2,4,128,128]{3,2,1,0:T(8,128)(2,1)} %pad_maximum_fusion), channel_id=1, source_target_pairs={{0,32},{8,40},{16,48},{24,56},{32,64},{40,72},{48,80},{56,88},{64,... | collective-permute-start | bytes 786440 | tf_op jit(solution)/shard_map/ppermute | solution.py:25
  147.3 0.7 copy-start.6
  148.0 13.0 %collective-permute-start.3 = (bf16[2,4,128,128]{3,2,1,0:T(8,128)(2,1)}, bf16[2,4,128,128]{3,2,1,0:T(8,128)(2,1)S(1)}, u32[]{:S(2)}, u32[]{:S(2)}) collective-permute-start(bf16[2,4,128,128]{3,2,1,0:T(8,128)(2,1)} %pad_maximum_fusion), channel_id=1, source_target_pairs={{0,8},{8,16},{16,24},{24,32},{32,40},{40,48},{48,56},{56,64},{64,7... | collective-permute-start | bytes 786440 | tf_op jit(solution)/shard_map/ppermute | solution.py:25
  150.9 21.7 %collective-permute-start.5 = (bf16[2,4,128,128]{3,2,1,0:T(8,128)(2,1)}, bf16[2,4,128,128]{3,2,1,0:T(8,128)(2,1)S(1)}, u32[]{:S(2)}, u32[]{:S(2)}) collective-permute-start(bf16[2,4,128,128]{3,2,1,0:T(8,128)(2,1)} %pad_maximum_fusion), channel_id=1, source_target_pairs={{16,0},{24,8},{32,16},{40,24},{48,32},{56,40},{64,48},{72,56},{80,... | collective-permute-start | bytes 786440 | tf_op jit(solution)/shard_map/ppermute | solution.py:25
  153.8 18.7 %collective-permute-start.4 = (bf16[2,4,128,128]{3,2,1,0:T(8,128)(2,1)}, bf16[2,4,128,128]{3,2,1,0:T(8,128)(2,1)S(1)}, u32[]{:S(2)}, u32[]{:S(2)}) collective-permute-start(bf16[2,4,128,128]{3,2,1,0:T(8,128)(2,1)} %pad_maximum_fusion), channel_id=1, source_target_pairs={{8,0},{16,8},{24,16},{32,24},{40,32},{48,40},{56,48},{64,56},{72,6... | collective-permute-start | bytes 786440 | tf_op jit(solution)/shard_map/ppermute | solution.py:25
  176.7 2.9 %copy-start.2 = (pred[4,128,16,128]{1,3,2,0:T(8,128)(4,1)S(1)}, pred[4,128,16,128]{1,3,2,0:T(8,128)(4,1)}, u32[]{:S(2)}) copy-start(pred[4,128,16,128]{1,3,2,0:T(8,128)(4,1)} %or_and_fusion) | copy-start | bytes 3145732
  176.7 2.9 %copy-start.5 = (bf16[4,128,4,128]{3,2,1,0:T(4,128)(2,1)S(1)}, bf16[4,128,4,128]{3,2,1,0:T(4,128)(2,1)}, u32[]{:S(2)}) copy-start(bf16[4,128,4,128]{3,2,1,0:T(4,128)(2,1)} %reshape.113) | copy-start | bytes 1572868
  179.6 2.6 %copy-start.3 = (bf16[4,16,2,128,128]{4,3,1,0,2:T(8,128)(2,1)}, bf16[4,16,2,128,128]{4,3,1,0,2:T(8,128)(2,1)S(1)}, u32[]{:S(2)}) copy-start(bf16[4,16,2,128,128]{4,3,1,0,2:T(8,128)(2,1)S(1)} %copy.59) | copy-start | bytes 12582916
  193.2 43.0 %copy-start.1 = (bf16[4096,128]{1,0:T(8,128)(2,1)S(1)}, bf16[4096,128]{1,0:T(8,128)(2,1)}, u32[]{:S(2)}) copy-start(bf16[4096,128]{1,0:T(8,128)(2,1)} %param.11) | copy-start | bytes 3145732
Sparse Core Ops, SparseCore 0:
  199.9 36.1 reduce-scatter.1
